TPU v7x, 32 devices: a whole 2x2x4 slice. The times are simulated.
32 devices in a mesh: dp: 4 (over z), vocab: 8 (over y, x, core).
Axes of the slice: x: 2, y: 2, z: 4, core: 2. Of those that a mesh axis runs over, the one named last changes fastest.
Arguments:
- base_hidden: bfloat16 [96, 8192], P('dp', 'vocab'), may hold values from -16 to 16
- reinforced_hidden: bfloat16 [96, 8192], P('dp', 'vocab'), may hold values from -16 to 16
- trained_hidden: bfloat16 [96, 8192], P('dp', 'vocab'), may hold values from -16 to 16
- frozen_head: bfloat16 [8192, 16384], P(None, ('dp', 'vocab')), may hold values from -1 to 1
- trained_head: bfloat16 [8192, 16384], P(None, ('dp', 'vocab')), may hold values from -1 to 1
- label_tokens: int32 [96], P('dp'), may hold values from 0 to 16383
- generic_map: int32 [16384], replicated, may hold values from 0 to 16383, as said below
- loss_mask: int32 [96], P('dp'), may hold values 0 or 1
Outputs:
- token_loss: float32 [96], P('dp')
- head_grad: bfloat16 [8192, 16384], P(None, ('dp', 'vocab'))
- hidden_grad: bfloat16 [96, 8192], P('dp', 'vocab')
Inputs may be any that keep to these rules, and one draw needn't show every extreme that they name: `generic_map`: maps each token to its generic counterpart; many tokens map to themselves.
All inputs are finite; a program needn't handle non-finite values. No bound on the sum of `loss_mask` on one device may be relied on, other than what follows from the above.
Results may differ from a plain program's by a relative error of at most 0.0065.
Values may be sent and summed in bfloat16 or wider, within the bound.
No kernel may reach another device: no remote copies, remote signals or barrier semaphores. Data moves between devices by JAX's collectives and lax.ppermute only.
A program may use at most 128 MiB of HBM per device.

v0:
```python
import jax
import jax.numpy as jnp
from jax import lax
from jax.sharding import PartitionSpec as P

reinforce_weight = 2.0
anchor_share = 0.3
loss_scale = 16.0


def on_device(
    base_hidden,
    reinforced_hidden,
    trained_hidden,
    frozen_head,
    trained_head,
    label_tokens,
    generic_map,
    loss_mask,
):
    tok_local = base_hidden.shape[0]
    feature_local = base_hidden.shape[1]
    dp_count = lax.axis_size("dp")
    vocab_count = lax.axis_size("vocab")
    wide_rows = (
        lax.all_gather(base_hidden, "vocab", axis=1, tiled=True),
        lax.all_gather(reinforced_hidden, "vocab", axis=1, tiled=True),
        lax.all_gather(trained_hidden, "vocab", axis=1, tiled=True),
    )
    base_rows, reinforced_rows, trained_rows = (
        lax.all_gather(wide_rows[0], "dp", axis=0, tiled=True),
        lax.all_gather(wide_rows[1], "dp", axis=0, tiled=True),
        lax.all_gather(wide_rows[2], "dp", axis=0, tiled=True),
    )
    all_labels = (
        lax.all_gather(label_tokens, "dp", axis=0, tiled=True),
        lax.all_gather(loss_mask, "dp", axis=0, tiled=True),
    )
    labels_all, mask_all = all_labels
    base_logits = jnp.dot(base_rows, frozen_head, preferred_element_type=jnp.float32)
    reinforced_logits = jnp.dot(reinforced_rows, frozen_head, preferred_element_type=jnp.float32)
    generic = base_logits - reinforce_weight * jnp.maximum(reinforced_logits - base_logits, 0.0)
    trained_logits = jnp.dot(trained_rows, trained_head, preferred_element_type=jnp.float32)
    vocab_local = trained_head.shape[1]
    vocab_start = lax.axis_index(("dp", "vocab")) * vocab_local
    anchor = generic_map[labels_all]
    anchor_hit = (vocab_start + lax.iota(jnp.int32, vocab_local))[None, :] == anchor[:, None]
    picked_local = jnp.sum(jnp.where(anchor_hit, trained_logits, 0.0), axis=1)
    generic_peak, trained_peak = lax.pmax(
        (jnp.max(generic, axis=1), jnp.max(trained_logits, axis=1)), ("dp", "vocab")
    )
    generic_exps = jnp.exp(generic - generic_peak[:, None])
    trained_exps = jnp.exp(trained_logits - trained_peak[:, None])
    generic_total, cross_term, trained_total, picked_logit = lax.psum(
        (
            jnp.sum(generic_exps, axis=1),
            jnp.sum(generic_exps * trained_logits, axis=1),
            jnp.sum(trained_exps, axis=1),
            picked_local,
        ),
        ("dp", "vocab"),
    )
    token_weight = mask_all.astype(jnp.float32)
    loss_all = token_weight * (
        trained_peak
        + jnp.log(trained_total)
        - (1.0 - anchor_share) * cross_term / generic_total
        - anchor_share * picked_logit
    )
    token_loss = lax.dynamic_slice_in_dim(loss_all, lax.axis_index("dp") * tok_local, tok_local, 0)
    target = (1.0 - anchor_share) * generic_exps / generic_total[
        :, None
    ] + anchor_share * anchor_hit.astype(jnp.float32)
    logit_grad = (
        loss_scale * token_weight[:, None] * (trained_exps / trained_total[:, None] - target)
    ).astype(jnp.bfloat16)
    head_total = lax.dot_general(
        trained_rows, logit_grad, (((0,), (0,)), ((), ())), preferred_element_type=jnp.float32
    )
    grad_blocks = logit_grad.reshape(dp_count, tok_local, vocab_local)
    head_blocks = trained_head.reshape(vocab_count, feature_local, vocab_local)
    hidden_terms = jnp.einsum(
        "atv,bdv->abtd", grad_blocks, head_blocks, preferred_element_type=jnp.float32
    )
    hidden_terms = hidden_terms.reshape(dp_count * vocab_count * tok_local, feature_local)
    hidden_total = lax.psum_scatter(hidden_terms, ("dp", "vocab"), scatter_dimension=0, tiled=True)
    return (token_loss, head_total.astype(jnp.bfloat16), hidden_total.astype(jnp.bfloat16))


def solution(mesh):
    placed = (
        P("dp", "vocab"),
        P("dp", "vocab"),
        P("dp", "vocab"),
        P(None, ("dp", "vocab")),
        P(None, ("dp", "vocab")),
        P("dp"),
        P(),
        P("dp"),
    )
    return jax.shard_map(
        on_device,
        mesh=mesh,
        in_specs=placed,
        out_specs=(P("dp"), P(None, ("dp", "vocab")), P("dp", "vocab")),
        check_vma=False,
    )
```

profile of v0, /device:TPU:0, one launch (start us, length us, event | category | flops | bytes accessed | tf_op | source)
XLA Modules:
  0.0 336.3 jit_solution(8015253757386036704)
XLA Ops:
  7.2 12.9 %all_gather.27 = bf16[24,8192]{1,0:T(8,128)(2,1)} all-gather(bf16[24,1024]{1,0:T(8,128)(2,1)} %param.8), channel_id=1, replica_groups=mesh['dp'=4,'vocab'=8] {'vocab'}, dimensions={1}, use_global_device_ids=true | all-gather | bytes 442368 | tf_op jit(solution)/shard_map/all_gather | solution.py:26
  20.2 10.5 %all_gather.29 = bf16[24,8192]{1,0:T(8,128)(2,1)} all-gather(bf16[24,1024]{1,0:T(8,128)(2,1)} %param.9), channel_id=1, replica_groups=mesh['dp'=4,'vocab'=8] {'vocab'}, dimensions={1}, use_global_device_ids=true | all-gather | bytes 442368 | tf_op jit(solution)/shard_map/all_gather | solution.py:27
  30.7 10.5 %all_gather.25 = bf16[24,8192]{1,0:T(8,128)(2,1)} all-gather(bf16[24,1024]{1,0:T(8,128)(2,1)} %param.10), channel_id=1, replica_groups=mesh['dp'=4,'vocab'=8] {'vocab'}, dimensions={1}, use_global_device_ids=true | all-gather | bytes 442368 | tf_op jit(solution)/shard_map/all_gather | solution.py:28
  41.3 1.2 dynamic-slice
  43.2 0.9 dynamic-update-slice.1
  44.1 0.8 dynamic-update-slice
  44.9 9.1 %all-reduce.2 = (s32[96]{0:T(128)S(1)}, s32[96]{0:T(128)S(1)}) all-reduce(s32[96]{0:T(128)S(1)} %dynamic-update-slice.1, s32[96]{0:T(128)S(1)} %dynamic-update-slice), channel_id=1, replica_groups=mesh['dp'=4,'vocab'=8] {'dp'}, use_global_device_ids=true, to_apply=%add.1 | all-reduce | flops 192 | bytes 1536
  54.1 1.1 gather_fusion
  55.2 2.5 all-gather.6.cloned.1.call-done
  57.8 5.3 %fusion.13 = f32[96,512]{1,0:T(8,128)S(1)} fusion(bf16[96,8192]{1,0:T(8,128)(2,1)} %all-gather.6.cloned.1.call-done, bf16[8192,512]{1,0:T(8,128)(2,1)} %param.11), kind=kOutput, calls=%fused_computation.26 | convolution fusion | flops 805306368 | bytes 10158080 | tf_op jit(solution)/shard_map/dot_general | solution.py:40
  63.1 32.2 %all-gather.8.cloned.1.call-done = bf16[96,8192]{1,0:T(8,128)(2,1)} async-done(((bf16[24,8192]{1,0:T(8,128)(2,1)}), bf16[96,8192]{1,0:T(8,128)(2,1)}) %all-gather.8.cloned.1.call-update) | async-done | bytes 1572880 | tf_op jit(solution)/shard_map/all_gather | solution.py:32
  95.3 5.4 %fusion.12 = (f32[96]{0:T(128)S(1)}, f32[96,512]{1,0:T(8,128)S(1)}) fusion(f32[96,512]{1,0:T(8,128)S(1)} %fusion.13, bf16[96,8192]{1,0:T(8,128)(2,1)} %all-gather.8.cloned.1.call-done, bf16[8192,512]{1,0:T(8,128)(2,1)} %param.11), kind=kOutput, calls=%fused_computation.25 | convolution fusion | flops 805552000 | bytes 10355072 | tf_op jit(solution)/shard_map/dot_general | solution.py:41
  100.7 32.1 %all-gather.4.cloned.1.call-done = bf16[96,8192]{1,0:T(8,128)(2,1)} async-done(((bf16[24,8192]{1,0:T(8,128)(2,1)}), bf16[96,8192]{1,0:T(8,128)(2,1)}) %all-gather.4.cloned.1.call-update) | async-done | bytes 1572880 | tf_op jit(solution)/shard_map/all_gather | solution.py:33
  132.8 5.4 %fusion.11 = (f32[96]{0:T(128)S(1)}, f32[96,512]{1,0:T(8,128)S(1)}) fusion(bf16[96,8192]{1,0:T(8,128)(2,1)} %all-gather.4.cloned.1.call-done, bf16[8192,512]{1,0:T(8,128)(2,1)} %param.12), kind=kOutput, calls=%fused_computation.24 | convolution fusion | flops 805355392 | bytes 10158464 | tf_op jit(solution)/shard_map/dot_general | solution.py:43
  138.2 39.2 %all-reduce.4 = (f32[96]{0:T(128)S(1)}, f32[96]{0:T(128)S(1)}) all-reduce(f32[96]{0:T(128)S(1)} %get-tuple-element.25, f32[96]{0:T(128)S(1)} %get-tuple-element.27), channel_id=1, replica_groups=mesh['dp'=4,'vocab'=8] {'dp','vocab'}, use_global_device_ids=true, to_apply=%region_1.2 | all-reduce | flops 192 | bytes 1536 | tf_op jit(solution)/shard_map/pmax | solution.py:49
  177.4 0.3 fusion.9
  177.7 40.1 %all-reduce.3 = (f32[96]{0:T(128)S(1)}, f32[96]{0:T(128)S(1)}, f32[96]{0:T(128)S(1)}, f32[96]{0:T(128)S(1)}) all-reduce(f32[96]{0:T(128)S(1)} %get-tuple-element.12, f32[96]{0:T(128)S(1)} %get-tuple-element.13, f32[96]{0:T(128)S(1)} %get-tuple-element.14, f32[96]{0:T(128)S(1)} %get-tuple-element.11), channel_id=1, replica_groups=mesh['dp'=4,'vocab'=8] {'dp','vocab'}, use_global_device_ids=true, to_apply=%region_11.12 | all-reduce | flops 384 | bytes 3072 | tf_op jit(solution)/shard_map/psum | solution.py:54
  217.8 0.2 fusion.8
  218.0 7.9 %fusion.14 = f32[4,24,8,1024]{3,1,2,0:T(8,128)} fusion(bf16[4,24,512,1]{2,1,3,0:T(8,128)(2,1)S(1)} %bitcast.26, bf16[8,1024,512,1]{2,1,0,3:T(8,128)(2,1)} %bitcast.24), kind=kOutput, calls=%fused_computation.27 | convolution fusion | flops 805306368 | bytes 11632640 | tf_op jit(solution)/shard_map/atv,bdv->abtd/dot_general | solution.py:82
  226.0 5.6 %fusion = bf16[8192,512]{0,1:T(8,128)(2,1)} fusion(bf16[96,512]{1,0:T(8,128)(2,1)S(1)} %fusion.8, bf16[96,8192]{1,0:T(8,128)(2,1)S(1)} %copy-done.1), kind=kOutput, calls=%fused_computation.2 | convolution fusion | flops 809500672 | bytes 10059776 | tf_op jit(solution)/shard_map/dot_general | solution.py:77
  231.5 12.0 %copy.12 = bf16[8192,512]{1,0:T(8,128)(2,1)} copy(bf16[8192,512]{0,1:T(8,128)(2,1)} %fusion) | data formatting | bytes 16777216
  243.6 0.6 dynamic_slice.3
  244.2 84.1 %reduce-scatter.2.cloned.1.call-done = f32[24,1024]{1,0:T(8,128)} async-done(((f32[768,1024]{1,0:T(8,128)}), f32[24,1024]{1,0:T(8,128)}) %reduce-scatter.2.cloned.1.call-update) | async-done | bytes 98320 | tf_op jit(solution)/shard_map/reduce_scatter | solution.py:86
  328.2 1.5 convert_element_type.20
  (18 shorter events, 0.3 us)
Async XLA Ops:
  7.2 46.9 %copy-start = (s32[16384]{0:T(1024)S(1)}, s32[16384]{0:T(1024)}, u32[]{:S(2)}) copy-start(s32[16384]{0:T(1024)} %param.14) | copy-start | bytes 196612
  7.2 50.6 %all-gather.6.cloned.1.call-start = ((), (), s32[]{:S(2)}) async-start(), calls=%async_computation.2 | async-start | bytes 1966080 | tf_op jit(solution)/shard_map/all_gather | solution.py:31
  20.2 75.1 %all-gather.8.cloned.1.call-start = ((), (), s32[]{:S(2)}) async-start(), calls=%async_computation.3 | async-start | bytes 1966080 | tf_op jit(solution)/shard_map/all_gather | solution.py:32
  30.7 102.1 %all-gather.4.cloned.1.call-start = ((), (), s32[]{:S(2)}) async-start(), calls=%async_computation.1 | async-start | bytes 1966080 | tf_op jit(solution)/shard_map/all_gather | solution.py:33
  41.2 287.0 %reduce-scatter.2.cloned.1.call-start = ((), (), s32[]{:S(2)}) async-start(), calls=%async_computation.4 | async-start | bytes 3244032 | tf_op jit(solution)/shard_map/reduce_scatter | solution.py:86
  218.0 8.0 %copy-start.1 = (bf16[96,8192]{1,0:T(8,128)(2,1)S(1)}, bf16[96,8192]{1,0:T(8,128)(2,1)}, u32[]{:S(2)}) copy-start(bf16[96,8192]{1,0:T(8,128)(2,1)} %all-gather.4.cloned.1.call-done) | copy-start | bytes 4718596
Sparse Core Ops, SparseCore 0:
  20.3 37.4 all-gather.5
  59.3 35.8 all-gather.7
  96.8 35.8 all-gather.3
  226.1 102.1 reduce-scatter.1
where the time goes:
time: 337 us; the launch traced here: 336 us
  waiting for transfers between devices  151 us (45%)
  blocking collectives  122 us (36%)
  matrix products  29.7 us (9%)
  local copies, waits for them, and re-layouts  16.7 us (5%)
  between operations  14.5 us (4%)
    reduce_scatter x1, waiting for transfers between devices, on_device(): lax.psum_scatter(hidden_terms, ('dp', 'vocab'), scatter_dimension=0, tile...  84.1 us
    psum x1, blocking collectives, on_device(): lax.psum((jnp.sum(generic_exps, axis=1), jnp.sum(generic_exps * trained_l...  40.1 us
    pmax x1, blocking collectives, on_device(): lax.pmax((jnp.max(generic, axis=1), jnp.max(trained_logits, axis=1)), ('d...  39.2 us
    all_gather x1, waiting for transfers between devices, on_device(): lax.all_gather(wide_rows[1], 'dp', axis=0, tiled=True)  32.2 us
    all_gather x1, waiting for transfers between devices, on_device(): lax.all_gather(wide_rows[2], 'dp', axis=0, tiled=True)  32.1 us
    unnamed x10, local copies, waits for them, and re-layouts  15 us
    all_gather x1, blocking collectives, on_device(): lax.all_gather(base_hidden, 'vocab', axis=1, tiled=True)  12.9 us
    all_gather x1, blocking collectives, on_device(): lax.all_gather(trained_hidden, 'vocab', axis=1, tiled=True)  10.5 us
  transfers between devices with their start and end apart: 4, of which 4 were waited for; matrix products, arithmetic and copies ran while one was open for 10% of the time, Pallas kernels for 0%

commit v1 on v0

--- a/solution.py
+++ b/solution.py
@@ -52,13 +52,16 @@
     generic_exps = jnp.exp(generic - generic_peak[:, None])
     trained_exps = jnp.exp(trained_logits - trained_peak[:, None])
     generic_total, cross_term, trained_total, picked_logit = lax.psum(
-        (
-            jnp.sum(generic_exps, axis=1),
-            jnp.sum(generic_exps * trained_logits, axis=1),
-            jnp.sum(trained_exps, axis=1),
-            picked_local,
+        lax.psum(
+            (
+                jnp.sum(generic_exps, axis=1),
+                jnp.sum(generic_exps * trained_logits, axis=1),
+                jnp.sum(trained_exps, axis=1),
+                picked_local,
+            ),
+            "vocab",
         ),
-        ("dp", "vocab"),
+        "dp",
     )
     token_weight = mask_all.astype(jnp.float32)
     loss_all = token_weight * (

time: 337 us -> 317 us (0.941)
  blocking collectives: 122 us -> 106 us
    psum x1, blocking collectives: 40.1 us -> 12.7 us  [on_device(): lax.psum((jnp.sum(generic_exps, axis=1), jnp.sum(generic_exps * trained_l...]
    psum x0 -> x1, blocking collectives: none -> 10.7 us  [on_device(): lax.psum(lax.psum((jnp.sum(generic_exps, axis=1), jnp.sum(generic_exps *...]
where the time goes in v1:
time: 317 us
  waiting for transfers between devices  148 us (47%)
  blocking collectives  106 us (33%)
  matrix products  29.7 us (9%)
  local copies, waits for them, and re-layouts  16.7 us (5%)
  between operations  14.5 us (5%)
    reduce_scatter x1, waiting for transfers between devices, on_device(): lax.psum_scatter(hidden_terms, ('dp', 'vocab'), scatter_dimension=0, tile...  81.1 us
    pmax x1, blocking collectives, on_device(): lax.pmax((jnp.max(generic, axis=1), jnp.max(trained_logits, axis=1)), ('d...  39.2 us
    all_gather x1, waiting for transfers between devices, on_device(): lax.all_gather(wide_rows[1], 'dp', axis=0, tiled=True)  32.2 us
    all_gather x1, waiting for transfers between devices, on_device(): lax.all_gather(wide_rows[2], 'dp', axis=0, tiled=True)  32.1 us
    unnamed x10, local copies, waits for them, and re-layouts  15 us
    all_gather x1, blocking collectives, on_device(): lax.all_gather(base_hidden, 'vocab', axis=1, tiled=True)  12.9 us
    psum x1, blocking collectives, on_device(): lax.psum((jnp.sum(generic_exps, axis=1), jnp.sum(generic_exps * trained_l...  12.7 us
    psum x1, blocking collectives, on_device(): lax.psum(lax.psum((jnp.sum(generic_exps, axis=1), jnp.sum(generic_exps *...  10.7 us
  transfers between devices with their start and end apart: 4, of which 4 were waited for; matrix products, arithmetic and copies ran while one was open for 10% of the time, Pallas kernels for 0%

profile of v1, /device:TPU:0, one launch (start us, length us, event | category | flops | bytes accessed | tf_op | source)
XLA Modules:
  0.0 316.6 jit_solution(8233436032974577527)
XLA Ops:
  7.2 12.9 %all_gather.27 = bf16[24,8192]{1,0:T(8,128)(2,1)} all-gather(bf16[24,1024]{1,0:T(8,128)(2,1)} %param.8), channel_id=1, replica_groups=mesh['dp'=4,'vocab'=8] {'vocab'}, dimensions={1}, use_global_device_ids=true | all-gather | bytes 442368 | tf_op jit(solution)/shard_map/all_gather | solution.py:26
  20.2 10.5 %all_gather.29 = bf16[24,8192]{1,0:T(8,128)(2,1)} all-gather(bf16[24,1024]{1,0:T(8,128)(2,1)} %param.9), channel_id=1, replica_groups=mesh['dp'=4,'vocab'=8] {'vocab'}, dimensions={1}, use_global_device_ids=true | all-gather | bytes 442368 | tf_op jit(solution)/shard_map/all_gather | solution.py:27
  30.7 10.5 %all_gather.25 = bf16[24,8192]{1,0:T(8,128)(2,1)} all-gather(bf16[24,1024]{1,0:T(8,128)(2,1)} %param.10), channel_id=1, replica_groups=mesh['dp'=4,'vocab'=8] {'vocab'}, dimensions={1}, use_global_device_ids=true | all-gather | bytes 442368 | tf_op jit(solution)/shard_map/all_gather | solution.py:28
  41.3 1.2 dynamic-slice
  43.2 0.9 dynamic-update-slice.1
  44.1 0.8 dynamic-update-slice
  44.9 9.1 %all-reduce.2 = (s32[96]{0:T(128)S(1)}, s32[96]{0:T(128)S(1)}) all-reduce(s32[96]{0:T(128)S(1)} %dynamic-update-slice.1, s32[96]{0:T(128)S(1)} %dynamic-update-slice), channel_id=1, replica_groups=mesh['dp'=4,'vocab'=8] {'dp'}, use_global_device_ids=true, to_apply=%add.1 | all-reduce | flops 192 | bytes 1536
  54.1 1.1 gather_fusion
  55.2 2.5 all-gather.6.cloned.1.call-done
  57.8 5.3 %fusion.13 = f32[96,512]{1,0:T(8,128)S(1)} fusion(bf16[96,8192]{1,0:T(8,128)(2,1)} %all-gather.6.cloned.1.call-done, bf16[8192,512]{1,0:T(8,128)(2,1)} %param.11), kind=kOutput, calls=%fused_computation.26 | convolution fusion | flops 805306368 | bytes 10158080 | tf_op jit(solution)/shard_map/dot_general | solution.py:40
  63.1 32.2 %all-gather.8.cloned.1.call-done = bf16[96,8192]{1,0:T(8,128)(2,1)} async-done(((bf16[24,8192]{1,0:T(8,128)(2,1)}), bf16[96,8192]{1,0:T(8,128)(2,1)}) %all-gather.8.cloned.1.call-update) | async-done | bytes 1572880 | tf_op jit(solution)/shard_map/all_gather | solution.py:32
  95.3 5.4 %fusion.12 = (f32[96]{0:T(128)S(1)}, f32[96,512]{1,0:T(8,128)S(1)}) fusion(f32[96,512]{1,0:T(8,128)S(1)} %fusion.13, bf16[96,8192]{1,0:T(8,128)(2,1)} %all-gather.8.cloned.1.call-done, bf16[8192,512]{1,0:T(8,128)(2,1)} %param.11), kind=kOutput, calls=%fused_computation.25 | convolution fusion | flops 805552000 | bytes 10355072 | tf_op jit(solution)/shard_map/dot_general | solution.py:41
  100.7 32.1 %all-gather.4.cloned.1.call-done = bf16[96,8192]{1,0:T(8,128)(2,1)} async-done(((bf16[24,8192]{1,0:T(8,128)(2,1)}), bf16[96,8192]{1,0:T(8,128)(2,1)}) %all-gather.4.cloned.1.call-update) | async-done | bytes 1572880 | tf_op jit(solution)/shard_map/all_gather | solution.py:33
  132.8 5.4 %fusion.11 = (f32[96]{0:T(128)S(1)}, f32[96,512]{1,0:T(8,128)S(1)}) fusion(bf16[96,8192]{1,0:T(8,128)(2,1)} %all-gather.4.cloned.1.call-done, bf16[8192,512]{1,0:T(8,128)(2,1)} %param.12), kind=kOutput, calls=%fused_computation.24 | convolution fusion | flops 805355392 | bytes 10158464 | tf_op jit(solution)/shard_map/dot_general | solution.py:43
  138.2 39.2 %all-reduce.3 = (f32[96]{0:T(128)S(1)}, f32[96]{0:T(128)S(1)}) all-reduce(f32[96]{0:T(128)S(1)} %get-tuple-element.29, f32[96]{0:T(128)S(1)} %get-tuple-element.31), channel_id=1, replica_groups=mesh['dp'=4,'vocab'=8] {'dp','vocab'}, use_global_device_ids=true, to_apply=%region_1.2 | all-reduce | flops 192 | bytes 1536 | tf_op jit(solution)/shard_map/pmax | solution.py:49
  177.4 0.3 fusion.9
  177.6 12.7 %all-reduce.4 = (f32[96]{0:T(128)S(1)}, f32[96]{0:T(128)S(1)}, f32[96]{0:T(128)S(1)}, f32[96]{0:T(128)S(1)}) all-reduce(f32[96]{0:T(128)S(1)} %get-tuple-element.12, f32[96]{0:T(128)S(1)} %get-tuple-element.13, f32[96]{0:T(128)S(1)} %get-tuple-element.14, f32[96]{0:T(128)S(1)} %get-tuple-element.11), channel_id=1, replica_groups=mesh['dp'=4,'vocab'=8] {'vocab'}, use_global_device_ids=true, to_apply=%region_14.15 | all-reduce | flops 384 | bytes 3072 | tf_op jit(solution)/shard_map/psum | solution.py:55
  190.3 10.7 %all-reduce.5 = (f32[96]{0:T(128)S(1)}, f32[96]{0:T(128)S(1)}, f32[96]{0:T(128)S(1)}, f32[96]{0:T(128)S(1)}) all-reduce(f32[96]{0:T(128)S(1)} %get-tuple-element.19, f32[96]{0:T(128)S(1)} %get-tuple-element.20, f32[96]{0:T(128)S(1)} %get-tuple-element.21, f32[96]{0:T(128)S(1)} %get-tuple-element.22), channel_id=1, replica_groups=mesh['dp'=4,'vocab'=8] {'dp'}, use_global_device_ids=true, to_apply=%region_15.16 | all-reduce | flops 384 | bytes 3072 | tf_op jit(solution)/shard_map/psum | solution.py:54
  201.2 7.9 %fusion.14 = f32[4,24,8,1024]{3,1,2,0:T(8,128)} fusion(bf16[4,24,512,1]{2,1,3,0:T(8,128)(2,1)S(1)} %bitcast.26, bf16[8,1024,512,1]{2,1,0,3:T(8,128)(2,1)} %bitcast.24), kind=kOutput, calls=%fused_computation.27 | convolution fusion | flops 805306368 | bytes 11632640 | tf_op jit(solution)/shard_map/atv,bdv->abtd/dot_general | solution.py:85
  209.2 5.6 %fusion = bf16[8192,512]{0,1:T(8,128)(2,1)} fusion(bf16[96,512]{1,0:T(8,128)(2,1)S(1)} %fusion.8, bf16[96,8192]{1,0:T(8,128)(2,1)S(1)} %copy-done.1), kind=kOutput, calls=%fused_computation.2 | convolution fusion | flops 809500672 | bytes 10059776 | tf_op jit(solution)/shard_map/dot_general | solution.py:80
  214.8 12.1 %copy.12 = bf16[8192,512]{1,0:T(8,128)(2,1)} copy(bf16[8192,512]{0,1:T(8,128)(2,1)} %fusion) | data formatting | bytes 16777216
  226.8 0.6 dynamic_slice.3
  227.4 81.1 %reduce-scatter.2.cloned.1.call-done = f32[24,1024]{1,0:T(8,128)} async-done(((f32[768,1024]{1,0:T(8,128)}), f32[24,1024]{1,0:T(8,128)}) %reduce-scatter.2.cloned.1.call-update) | async-done | bytes 98320 | tf_op jit(solution)/shard_map/reduce_scatter | solution.py:89
  308.6 1.5 convert_element_type.20
  (19 shorter events, 0.5 us)
Async XLA Ops:
  7.2 46.9 %copy-start = (s32[16384]{0:T(1024)S(1)}, s32[16384]{0:T(1024)}, u32[]{:S(2)}) copy-start(s32[16384]{0:T(1024)} %param.14) | copy-start | bytes 196612
  7.2 50.6 %all-gather.6.cloned.1.call-start = ((), (), s32[]{:S(2)}) async-start(), calls=%async_computation.2 | async-start | bytes 1966080 | tf_op jit(solution)/shard_map/all_gather | solution.py:31
  20.2 75.1 %all-gather.8.cloned.1.call-start = ((), (), s32[]{:S(2)}) async-start(), calls=%async_computation.3 | async-start | bytes 1966080 | tf_op jit(solution)/shard_map/all_gather | solution.py:32
  30.7 102.1 %all-gather.4.cloned.1.call-start = ((), (), s32[]{:S(2)}) async-start(), calls=%async_computation.1 | async-start | bytes 1966080 | tf_op jit(solution)/shard_map/all_gather | solution.py:33
  41.2 267.3 %reduce-scatter.2.cloned.1.call-start = ((), (), s32[]{:S(2)}) async-start(), calls=%async_computation.4 | async-start | bytes 3244032 | tf_op jit(solution)/shard_map/reduce_scatter | solution.py:89
  201.2 8.0 %copy-start.1 = (bf16[96,8192]{1,0:T(8,128)(2,1)S(1)}, bf16[96,8192]{1,0:T(8,128)(2,1)}, u32[]{:S(2)}) copy-start(bf16[96,8192]{1,0:T(8,128)(2,1)} %all-gather.4.cloned.1.call-done) | copy-start | bytes 4718596
Sparse Core Ops, SparseCore 0:
  20.3 37.4 all-gather.5
  59.3 35.8 all-gather.7
  96.8 35.8 all-gather.3
  209.3 99.2 reduce-scatter.1
